TPU v7x, 128 devices: a whole 4x4x4 slice. The times are simulated.
128 devices in a mesh: row: 8 (over y, core), col: 16 (over x, z).
Axes of the slice: x: 4, y: 4, z: 4, core: 2. Of those that a mesh axis runs over, the one named last changes fastest.
Arguments:
- contribution: float32 [8, 8, 4, 16, 128, 128], P(None, 'row', None, 'col'), may hold values from -6 to 6
- parent_tiles: float32 [16, 8, 8, 16, 128, 128], P(None, 'row', None, 'col'), may hold values from -6 to 6
- row_basis: float32 [8, 8, 64, 128], P(None, 'row'), may hold values from -2.4 to 2.4
- pivot_basis: float32 [8, 8, 64, 2048], P(None, 'row', None, 'col'), may hold values from -0.125 to 0.125
- tile_ranks: int32 [64], replicated, may hold values from 16 to 64, as said below
- block_map: int32 [64], replicated, may hold values from 0 to 127, as said below
- panel_start: int32 [1], replicated, may hold values from 0 to 63
- pivot_inverse: float32 [512, 512], replicated
Outputs:
- updated_parent: float32 [16, 8, 8, 16, 128, 128], P(None, 'row', None, 'col')
Inputs may be any that keep to these rules, and one draw needn't show every extreme that they name: `tile_ranks`: multiples of 16; both 16 and 64 occur. `block_map`: child tile row u * 16 + l, for 0 <= l < 16, maps to parent tile row 2 * 16 * u + h_u + l with 0 <= h_u < 16; the 4 values h_u are distinct modulo 8.
All inputs are finite; a program needn't handle non-finite values.
Results may differ from a plain program's by a relative error of at most 0.0003.
Values sent between devices are 32-bit elements; how exact they have to be, the bound alone decides.
No kernel may reach another device: no remote copies, remote signals or barrier semaphores. Data moves between devices by JAX's collectives and lax.ppermute only.
A program may use at most 128 MiB of HBM per device.

v0:
```python
import jax
import jax.numpy as jnp
from jax import lax
from jax.sharding import PartitionSpec as P

PANEL_T = 4
highest = lax.Precision.HIGHEST


def spread_2(x, axis, root):
    mine = lax.axis_index(axis) == root
    return lax.psum(jnp.where(mine, x, jnp.zeros_like(x)), axis)


def from_behind(x, axis, by):
    count = lax.axis_size(axis)
    return lax.ppermute(x, axis, [(i, (i + by) % count) for i in range(count)])


def select_entries(lookup, wanted):
    matches = wanted[:, None] == jnp.arange(lookup.shape[0], dtype=jnp.int32)[None, :]
    return jnp.sum(jnp.where(matches, lookup[None, :], 0), axis=1)


def keep_ranks(factor, tile_index, rank_table):
    limits = select_entries(rank_table, tile_index)
    kept_cols = (jnp.arange(factor.shape[1], dtype=jnp.int32)[None, :] < limits[:, None]).astype(
        jnp.float32
    )
    return factor * kept_cols[:, :, None]


def every_other(stacked, groups, offset):
    shaped = stacked.reshape((groups, stacked.shape[0] // groups) + stacked.shape[1:])
    return lax.dynamic_index_in_dim(shaped, offset, axis=1, keepdims=False)


def per_device(
    contribution,
    parent_tiles,
    row_basis,
    pivot_basis,
    tile_ranks,
    block_map,
    panel_start,
    pivot_inverse,
):
    rows_grid = lax.axis_size("row")
    cols_grid = lax.axis_size("col")
    my_row = lax.axis_index("row")
    my_col = lax.axis_index("col")
    local_rows = contribution.shape[0]
    local_cols = contribution.shape[2]
    parent_rows = parent_tiles.shape[0]
    parent_cols = parent_tiles.shape[2]
    rank_max = row_basis.shape[2]
    per_block = cols_grid // rows_grid
    row_index = jnp.arange(local_rows, dtype=jnp.int32) * rows_grid + my_row
    col_index = jnp.arange(local_cols, dtype=jnp.int32) * cols_grid + my_col
    root_row = my_col % rows_grid
    offset = my_col // rows_grid
    own_basis = keep_ranks(row_basis[:, 0], row_index, tile_ranks)
    own_pivots = pivot_basis[:, 0]
    basis_picked = every_other(row_basis[:, 0], local_cols, offset)
    col_basis = spread_2(basis_picked, "row", root_row)
    all_pivots = lax.all_gather(pivot_basis, "row", axis=1, tiled=True)
    pivot_width = pivot_basis.shape[3]
    grouped = all_pivots.reshape(local_cols, cols_grid, rank_max, pivot_width)
    products = jnp.einsum(
        "trp,scup->cstru",
        own_pivots,
        grouped,
        precision=highest,
        preferred_element_type=jnp.float32,
    )
    weights = lax.psum_scatter(
        products.reshape(lax.axis_size("col") * local_cols, local_rows, rank_max * rank_max),
        "col",
        scatter_dimension=0,
        tiled=True,
    )
    weights = weights.reshape(local_cols, local_rows, rank_max, rank_max)
    col_basis = keep_ranks(col_basis, col_index, tile_ranks)
    half_product = jnp.einsum(
        "trx,stru->tsux", own_basis, weights, precision=highest, preferred_element_type=jnp.float32
    )
    update = jnp.einsum(
        "tsux,suy->tsxy",
        half_product,
        col_basis,
        precision=highest,
        preferred_element_type=jnp.float32,
    )
    lower_mask = (row_index[:, None] >= col_index[None, :])[:, :, None, None]
    payload = jnp.where(lower_mask, contribution[:, 0, :, 0] - update, jnp.float32(0.0))
    block_first = jnp.arange(local_cols, dtype=jnp.int32) * cols_grid
    shifts = select_entries(block_map, block_first) - 2 * block_first
    row_shift = jnp.repeat(shifts, per_block) % rows_grid
    for bit_index in range((rows_grid - 1).bit_length()):
        arrived = from_behind(payload, "row", 1 << bit_index)
        taken = row_shift // (1 << bit_index) % 2 == 1
        payload = jnp.where(taken[:, None, None, None], arrived, payload)
    for bit_index in range((cols_grid - 1).bit_length()):
        arrived = from_behind(payload, "col", 1 << bit_index)
        taken = shifts // (1 << bit_index) % 2 == 1
        payload = jnp.where(taken[None, :, None, None], arrived, payload)
    row_source = (my_row - row_shift) % rows_grid
    target_rows = (
        select_entries(block_map, jnp.arange(local_rows, dtype=jnp.int32) * rows_grid + row_source)
        // rows_grid
    )
    col_source = (my_col - shifts) % cols_grid
    target_cols = (
        select_entries(block_map, jnp.arange(local_cols, dtype=jnp.int32) * cols_grid + col_source)
        // cols_grid
    )
    row_place = (jnp.arange(parent_rows, dtype=jnp.int32)[:, None] == target_rows[None, :]).astype(
        jnp.float32
    )
    col_place = (jnp.arange(parent_cols, dtype=jnp.int32)[:, None] == target_cols[None, :]).astype(
        jnp.float32
    )
    spread = jnp.einsum(
        "at,tsxy->asxy", row_place, payload, precision=highest, preferred_element_type=jnp.float32
    )
    spread = jnp.einsum(
        "bs,asxy->abxy", col_place, spread, precision=highest, preferred_element_type=jnp.float32
    )
    assembled = parent_tiles[:, 0, :, 0] + spread
    start_col = panel_start[0]
    panel_parts = []
    for panel_index in range(PANEL_T):
        column_id = start_col + panel_index
        column = lax.dynamic_index_in_dim(assembled, column_id // cols_grid, axis=1, keepdims=False)
        panel_parts.append(spread_2(column, "col", column_id % cols_grid))
    row_panel = jnp.concatenate(panel_parts, axis=2)
    col_panel = spread_2(every_other(row_panel, parent_cols, offset), "row", root_row)
    scaled = jnp.einsum(
        "axp,pq->axq",
        row_panel,
        pivot_inverse,
        precision=highest,
        preferred_element_type=jnp.float32,
    )
    trailing = jnp.einsum(
        "axq,byq->abxy", scaled, col_panel, precision=highest, preferred_element_type=jnp.float32
    )
    big_rows = jnp.arange(parent_rows, dtype=jnp.int32) * rows_grid + my_row
    big_cols = jnp.arange(parent_cols, dtype=jnp.int32) * cols_grid + my_col
    window = (big_rows[:, None] >= big_cols[None, :]) & (big_cols[None, :] >= start_col + PANEL_T)
    result = jnp.where(window[:, :, None, None], assembled - trailing, assembled)
    return result[:, None, :, None]


def solution(mesh):
    placed = (
        P(None, "row", None, "col", None, None),
        P(None, "row", None, "col", None, None),
        P(None, "row", None, None),
        P(None, "row", None, "col"),
        P(),
        P(),
        P(),
        P(),
    )
    return jax.shard_map(
        per_device,
        mesh=mesh,
        in_specs=placed,
        out_specs=P(None, "row", None, "col", None, None),
        check_vma=False,
    )
```

profile of v0, /device:TPU:0, one launch (start us, length us, event | category | flops | bytes accessed | tf_op | source)
XLA Modules:
  0.0 810.4 jit_solution(2350074608308215927)
XLA Ops:
  6.5 0.7 all-gather.2.cloned.1.call-update
  7.3 29.4 %all-gather.2.cloned.1.call-done = f32[8,8,64,128]{3,2,1,0:T(8,128)} async-done(((f32[8,1,64,128]{3,2,1,0:T(8,128)}), f32[8,8,64,128]{3,2,1,0:T(8,128)}) %all-gather.2.cloned.1.call-update) | async-done | bytes 2097168 | tf_op jit(solution)/shard_map/all_gather | solution.py:66
  36.7 17.0 %convolution_bitcast_fusion = f32[16,4,8,64,64]{3,4,2,0,1:T(8,128)} fusion(f32[4,16,64,128,1]{3,2,4,1,0:T(8,128)} %bitcast.109, f32[8,1,64,128]{3,2,1,0:T(8,128)} %param.11), kind=kOutput, calls=%fused_computation.1 | convolution fusion | flops 3221225472 | bytes 10747904 | tf_op jit(solution)/shard_map/trp,scup->cstru/dot_general | solution.py:69
  53.7 17.6 %copy.33 = f32[16,4,8,64,64]{4,3,2,1,0:T(8,128)} copy(f32[16,4,8,64,64]{3,4,2,0,1:T(8,128)} %convolution_bitcast_fusion) | data formatting | bytes 16777216 | tf_op jit(solution)/shard_map/trp,scup->cstru/transpose | solution.py:69
  71.3 14.7 %reshape.468 = f32[64,8,4096]{2,1,0:T(8,128)} reshape(f32[16,4,8,64,64]{4,3,2,1,0:T(8,128)} %copy.33) | data formatting | bytes 16777216 | tf_op jit(solution)/shard_map/reshape | solution.py:77
  86.2 0.8 copy-done.7
  87.0 0.7 fusion.15
  88.4 1.8 copy.31
  90.2 81.4 %reduce-scatter.2.cloned.1.call-done = f32[4,8,4096]{2,1,0:T(8,128)} async-done(((f32[64,8,4096]{2,1,0:T(8,128)}), f32[4,8,4096]{2,1,0:T(8,128)}) %reduce-scatter.2.cloned.1.call-update) | async-done | bytes 524304 | tf_op jit(solution)/shard_map/reduce_scatter | solution.py:76
  171.7 1.5 reshape.469
  173.1 2.9 fusion.13
  176.0 56.6 %all-reduce.5.cloned.1.call-done = f32[4,64,128]{2,1,0:T(8,128)} async-done(((f32[4,64,128]{2,1,0:T(8,128)}), f32[4,64,128]{2,1,0:T(8,128)}) %all-reduce.5.cloned.1.call-update) | async-done | bytes 131088 | tf_op jit(solution)/shard_map/psum | solution.py:12
  232.6 3.9 fusion.9
  237.0 26.3 %collective-permute-done = f32[8,4,128,128]{2,3,0,1:T(8,128)} collective-permute-done((f32[8,4,128,128]{2,3,0,1:T(8,128)S(1)}, f32[8,4,128,128]{2,3,0,1:T(8,128)}, u32[]{:S(2)}, u32[]{:S(2)}) %collective-permute-start) | collective-permute-done | bytes 2097184 | tf_op jit(solution)/shard_map/ppermute | solution.py:17
  263.4 1.9 broadcast_select_fusion.1
  265.3 45.3 %collective-permute-done.1 = f32[8,4,128,128]{2,3,0,1:T(8,128)S(1)} collective-permute-done((f32[8,4,128,128]{2,3,0,1:T(8,128)S(1)}, f32[8,4,128,128]{2,3,0,1:T(8,128)S(1)}, u32[]{:S(2)}, u32[]{:S(2)}) %collective-permute-start.1) | collective-permute-done | bytes 2097184 | tf_op jit(solution)/shard_map/ppermute | solution.py:17
  310.7 0.4 broadcast_select_fusion.2
  311.1 0.8 collective-permute-start.2
  311.9 45.3 %collective-permute-done.2 = f32[8,4,128,128]{2,3,0,1:T(8,128)S(1)} collective-permute-done((f32[8,4,128,128]{2,3,0,1:T(8,128)S(1)}, f32[8,4,128,128]{2,3,0,1:T(8,128)S(1)}, u32[]{:S(2)}, u32[]{:S(2)}) %collective-permute-start.2) | collective-permute-done | bytes 2097184 | tf_op jit(solution)/shard_map/ppermute | solution.py:17
  357.2 0.4 broadcast_select_fusion.3
  357.6 2.1 collective-permute-start.3
  359.7 47.1 %collective-permute-done.3 = f32[8,4,128,128]{2,3,0,1:T(8,128)S(1)} collective-permute-done((f32[8,4,128,128]{2,3,0,1:T(8,128)S(1)}, f32[8,4,128,128]{2,3,0,1:T(8,128)S(1)}, u32[]{:S(2)}, u32[]{:S(2)}) %collective-permute-start.3) | collective-permute-done | bytes 2097184 | tf_op jit(solution)/shard_map/ppermute | solution.py:17
  406.8 0.4 broadcast_select_fusion.4
  407.3 49.8 %collective-permute-done.4 = f32[8,4,128,128]{2,3,0,1:T(8,128)S(1)} collective-permute-done((f32[8,4,128,128]{2,3,0,1:T(8,128)S(1)}, f32[8,4,128,128]{2,3,0,1:T(8,128)S(1)}, u32[]{:S(2)}, u32[]{:S(2)}) %collective-permute-start.4) | collective-permute-done | bytes 2097184 | tf_op jit(solution)/shard_map/ppermute | solution.py:17
  457.1 0.4 broadcast_select_fusion.5
  457.6 65.4 %collective-permute-done.5 = f32[8,4,128,128]{2,3,0,1:T(8,128)S(1)} collective-permute-done((f32[8,4,128,128]{2,3,0,1:T(8,128)S(1)}, f32[8,4,128,128]{2,3,0,1:T(8,128)S(1)}, u32[]{:S(2)}, u32[]{:S(2)}) %collective-permute-start.5) | collective-permute-done | bytes 2097184 | tf_op jit(solution)/shard_map/ppermute | solution.py:17
  522.9 0.3 broadcast_select_fusion.6
  524.5 26.5 %collective-permute-done.6 = f32[8,4,128,128]{2,3,0,1:T(8,128)} collective-permute-done((f32[8,4,128,128]{2,3,0,1:T(8,128)S(1)}, f32[8,4,128,128]{2,3,0,1:T(8,128)}, u32[]{:S(2)}, u32[]{:S(2)}) %collective-permute-start.6) | collective-permute-done | bytes 2097184 | tf_op jit(solution)/shard_map/ppermute | solution.py:17
  551.0 3.2 broadcast_select_fusion.7
  554.2 2.0 copy.35
  556.3 1.9 fusion.21
  558.2 13.0 %bitcast_add_fusion = f32[16,8,128,128]{3,1,2,0:T(8,128)S(1)} fusion(f32[16,1,8,1,128,128]{5,4,3,2,1,0:T(8,128)} %param.9, f32[16,4,128,128]{3,0,2,1:T(8,128)S(1)} %fusion.21, s32[4]{0:T(128)S(1)} %and_select_fusion), kind=kOutput, calls=%fused_computation.3 | convolution fusion | flops 102760480 | bytes 20971536 | tf_op jit(solution)/shard_map/bs,asxy->abxy/dot_general | solution.py:126
  571.2 1.2 broadcast.768
  572.4 5.8 broadcast_select_fusion
  578.2 1.1 select_bitcast_fusion.2
  579.3 1.6 select_bitcast_fusion
  580.9 0.2 all-reduce.7.cloned.1.call-start
  581.1 104.7 %all-reduce.9.cloned.1.call-done = (f32[16,128,128]{2,1,0:T(8,128)}, f32[16,128,128]{2,1,0:T(8,128)}, f32[16,128,128]{2,1,0:T(8,128)}, f32[16,128,128]{2,1,0:T(8,128)}) async-done(((f32[16,128,128]{2,1,0:T(8,128)}, f32[16,128,128]{2,1,0:T(8,128)}, f32[16,128,128]{2,1,0:T(8,128)}, f32[16,128,128]{2,1,0:T(8,128)}), (f32[16,128,128]{2,1,0:T(8,128)}, f32[16,128,128]{2,1,0:T(8,128)}, f32[16,128,128]{2,1,0:T(8,128)}, ...) | async-done | bytes 4194320 | tf_op jit(solution)/shard_map/psum | solution.py:12
  685.8 1.5 constant_dynamic-update-slice_fusion.3
  687.8 0.9 copy-done.4
  688.8 1.9 copy-done.2
  690.8 1.6 fusion.7
  692.5 9.9 %fusion.10 = f32[16,128,512]{2,1,0:T(8,128)} fusion(f32[16,128,512]{2,1,0:T(8,128)} %copy-done.2, f32[512,512]{1,0:T(8,128)S(1)} %copy-done), kind=kOutput, calls=%fused_computation.14 | convolution fusion | flops 6442450944 | bytes 9437184 | tf_op jit(solution)/shard_map/axp,pq->axq/dot_general | solution.py:138
  702.4 55.5 %all-reduce.7.cloned.1.call-done = f32[8,128,512]{2,1,0:T(8,128)} async-done(((f32[8,128,512]{2,1,0:T(8,128)}), f32[8,128,512]{2,1,0:T(8,128)}) %all-reduce.7.cloned.1.call-update) | async-done | bytes 2097168 | tf_op jit(solution)/shard_map/psum | solution.py:12
  757.9 18.0 %fusion.1 = f32[8,128,16,128]{3,1,2,0:T(8,128)} fusion(f32[16,128,512]{2,1,0:T(8,128)} %fusion.10, f32[8,128,512]{2,1,0:T(8,128)} %all-reduce.7.cloned.1.call-done), kind=kOutput, calls=%fused_computation.4 | convolution fusion | flops 12884901888 | bytes 14680064 | tf_op jit(solution)/shard_map/axq,byq->abxy/dot_general | solution.py:145
  775.9 9.4 %copy.42 = f32[8,128,16,128]{1,0,3,2:T(8,128)} copy(f32[8,128,16,128]{3,1,2,0:T(8,128)} %fusion.1) | data formatting | bytes 16777216 | tf_op jit(solution)/shard_map/axq,byq->abxy/dot_general | solution.py:145
  785.3 10.2 %fusion = f32[16,1,8,1,128,128]{5,2,4,0,3,1:T(8,128)} fusion(f32[16,8,128,128]{3,1,2,0:T(8,128)} %copy-done.1, f32[8,128,16,128]{1,0,3,2:T(8,128)} %copy.42, pred[16,8]{1,0:T(8,128)(4,1)S(1)} %compare_and_fusion), kind=kLoop, calls=%fused_computation.2 | loop fusion | flops 4194304 | bytes 25165952 | tf_op jit(solution)/shard_map/broadcast_in_dim | solution.py:152
  795.4 8.2 %copy.43 = f32[16,1,8,1,128,128]{5,4,3,2,1,0:T(8,128)} copy(f32[16,1,8,1,128,128]{5,2,4,0,3,1:T(8,128)} %fusion) | data formatting | bytes 16777216 | tf_op jit(solution)/shard_map/broadcast_in_dim | solution.py:152
  (56 shorter events, 2.6 us)
Async XLA Ops:
  6.5 686.0 %copy-start = (f32[512,512]{1,0:T(8,128)S(1)}, f32[512,512]{1,0:T(8,128)}, u32[]{:S(2)}) copy-start(f32[512,512]{1,0:T(8,128)} %param.15) | copy-start | bytes 3145732
  6.5 30.2 %all-gather.2.cloned.1.call-start = ((), (), s32[]{:S(2)}) async-start(), calls=%async_computation.2 | async-start | bytes 2359296 | tf_op jit(solution)/shard_map/all_gather | solution.py:66
  7.3 164.4 %reduce-scatter.2.cloned.1.call-start = ((), (), s32[]{:S(2)}) async-start(), calls=%async_computation.3 | async-start | bytes 8912896 | tf_op jit(solution)/shard_map/reduce_scatter | solution.py:76
  86.1 0.9 copy-start.7
  86.1 1.8 copy-start.8
  86.1 2.3 copy-start.3
  86.1 146.5 %all-reduce.5.cloned.1.call-start = ((), (), s32[]{:S(2)}) async-start(), calls=%async_computation.1 | async-start | bytes 262144 | tf_op jit(solution)/shard_map/psum | solution.py:12
  87.7 598.1 %all-reduce.9.cloned.1.call-start = ((), (), s32[]{:S(2)}) async-start(), calls=%async_computation.5 | async-start | bytes 8388608 | tf_op jit(solution)/shard_map/psum | solution.py:12
  176.0 60.6 %copy-start.9 = (s32[64]{0:T(128)S(1)}, s32[64]{0:T(128)}, u32[]{:S(2)}) copy-start(s32[64]{0:T(128)} %param.13) | copy-start | bytes 772
  236.6 26.8 %collective-permute-start = (f32[8,4,128,128]{2,3,0,1:T(8,128)S(1)}, f32[8,4,128,128]{2,3,0,1:T(8,128)}, u32[]{:S(2)}, u32[]{:S(2)}) collective-permute-start(f32[8,4,128,128]{2,3,0,1:T(8,128)S(1)} %fusion.9), channel_id=1, source_target_pairs={{0,16},{16,32},{32,48},{48,64},{64,80},{80,96},{96,112},{112,0},{1... | collective-permute-start | bytes 6291464 | tf_op jit(solution)/shard_map/ppermute | solution.py:17
  265.3 45.4 %collective-permute-start.1 = (f32[8,4,128,128]{2,3,0,1:T(8,128)S(1)}, f32[8,4,128,128]{2,3,0,1:T(8,128)S(1)}, u32[]{:S(2)}, u32[]{:S(2)}) collective-permute-start(f32[8,4,128,128]{2,3,0,1:T(8,128)S(1)} %broadcast_select_fusion.1), channel_id=1, source_target_pairs={{0,32},{16,48},{32,64},{48,80},{64,96},{80,112},{96,0},{112,16},{1... | collective-permute-start | bytes 6291464 | tf_op jit(solution)/shard_map/ppermute | solution.py:17
  311.1 46.1 %collective-permute-start.2 = (f32[8,4,128,128]{2,3,0,1:T(8,128)S(1)}, f32[8,4,128,128]{2,3,0,1:T(8,128)S(1)}, u32[]{:S(2)}, u32[]{:S(2)}) collective-permute-start(f32[8,4,128,128]{2,3,0,1:T(8,128)S(1)} %broadcast_select_fusion.2), channel_id=1, source_target_pairs={{0,64},{16,80},{32,96},{48,112},{64,0},{80,16},{96,32},{112,48},{1... | collective-permute-start | bytes 6291464 | tf_op jit(solution)/shard_map/ppermute | solution.py:17
  357.6 49.2 %collective-permute-start.3 = (f32[8,4,128,128]{2,3,0,1:T(8,128)S(1)}, f32[8,4,128,128]{2,3,0,1:T(8,128)S(1)}, u32[]{:S(2)}, u32[]{:S(2)}) collective-permute-start(f32[8,4,128,128]{2,3,0,1:T(8,128)S(1)} %broadcast_select_fusion.3), channel_id=1, source_target_pairs={{0,1},{1,2},{2,3},{3,4},{4,5},{5,6},{6,7},{7,8},{8,9},{9,10},{10,1... | collective-permute-start | bytes 6291464 | tf_op jit(solution)/shard_map/ppermute | solution.py:17
  407.2 49.9 %collective-permute-start.4 = (f32[8,4,128,128]{2,3,0,1:T(8,128)S(1)}, f32[8,4,128,128]{2,3,0,1:T(8,128)S(1)}, u32[]{:S(2)}, u32[]{:S(2)}) collective-permute-start(f32[8,4,128,128]{2,3,0,1:T(8,128)S(1)} %broadcast_select_fusion.4), channel_id=1, source_target_pairs={{0,2},{1,3},{2,4},{3,5},{4,6},{5,7},{6,8},{7,9},{8,10},{9,11},{10,... | collective-permute-start | bytes 6291464 | tf_op jit(solution)/shard_map/ppermute | solution.py:17
  457.5 65.5 %collective-permute-start.5 = (f32[8,4,128,128]{2,3,0,1:T(8,128)S(1)}, f32[8,4,128,128]{2,3,0,1:T(8,128)S(1)}, u32[]{:S(2)}, u32[]{:S(2)}) collective-permute-start(f32[8,4,128,128]{2,3,0,1:T(8,128)S(1)} %broadcast_select_fusion.5), channel_id=1, source_target_pairs={{0,4},{1,5},{2,6},{3,7},{4,8},{5,9},{6,10},{7,11},{8,12},{9,13},{1... | collective-permute-start | bytes 6291464 | tf_op jit(solution)/shard_map/ppermute | solution.py:17
  523.3 27.7 %collective-permute-start.6 = (f32[8,4,128,128]{2,3,0,1:T(8,128)S(1)}, f32[8,4,128,128]{2,3,0,1:T(8,128)}, u32[]{:S(2)}, u32[]{:S(2)}) collective-permute-start(f32[8,4,128,128]{2,3,0,1:T(8,128)S(1)} %broadcast_select_fusion.6), channel_id=1, source_target_pairs={{0,8},{1,9},{2,10},{3,11},{4,12},{5,13},{6,14},{7,15},{8,0},{9,1},... | collective-permute-start | bytes 6291464 | tf_op jit(solution)/shard_map/ppermute | solution.py:17
  571.2 7.0 copy-start.1
  580.9 177.0 %all-reduce.7.cloned.1.call-start = ((), (), s32[]{:S(2)}) async-start(), calls=%async_computation.4 | async-start | bytes 4194304 | tf_op jit(solution)/shard_map/psum | solution.py:12
  685.8 1.5 copy-start.6
  685.8 1.9 copy-start.5
  687.4 1.3 copy-start.4
  688.8 2.0 copy-start.2
Sparse Core Ops, SparseCore 0:
  9.1 27.6 all-gather.1
  86.2 85.3 reduce-scatter.1
  174.0 58.6 all-reduce.4
  581.0 104.7 all-reduce.8
  692.5 65.3 all-reduce.6
where the time goes:
time: 820 us; the launch traced here: 810 us
  waiting for transfers between devices  634 us (77%)
  matrix products  66.6 us (8%)
  local copies, waits for them, and re-layouts  62.5 us (8%)
  other arithmetic  29.3 us (4%)
  between operations  14.4 us (2%)
    ppermute x7, waiting for transfers between devices, from_behind(): return lax.ppermute(x, axis, [(i, (i + by) % count) for i in range(count)])  306 us
    psum x3, waiting for transfers between devices, spread_2(): return lax.psum(jnp.where(mine, x, jnp.zeros_like(x)), axis)  217 us
    reduce_scatter x1, waiting for transfers between devices, per_device(): lax.psum_scatter(products.reshape(lax.axis_size('col') * local_cols, loca...  81.4 us
    all_gather x1, waiting for transfers between devices, per_device(): all_pivots = lax.all_gather(pivot_basis, 'row', axis=1, tiled=True)  29.4 us
    dot_general x1, matrix products, per_device(): jnp.einsum('axq,byq->abxy', scaled, col_panel, precision=highest, preferr...  18 us
    transpose x1, local copies, waits for them, and re-layouts, per_device(): jnp.einsum('trp,scup->cstru', own_pivots, grouped, precision=highest, pre...  17.6 us
    dot_general x1, matrix products, per_device(): jnp.einsum('trp,scup->cstru', own_pivots, grouped, precision=highest, pre...  17 us
  transfers between devices with their start and end apart: 12, of which 12 were waited for; matrix products, arithmetic and copies ran while one was open for 2% of the time, Pallas kernels for 0%

commit v1 on v0

--- a/solution.py
+++ b/solution.py
@@ -63,7 +63,11 @@
     own_pivots = pivot_basis[:, 0]
     basis_picked = every_other(row_basis[:, 0], local_cols, offset)
     col_basis = spread_2(basis_picked, "row", root_row)
-    all_pivots = lax.all_gather(pivot_basis, "row", axis=1, tiled=True)
+    size = lax.axis_size("row")
+    repeats = [size if d == 1 else 1 for d in range(pivot_basis.ndim)]
+    all_pivots = lax.all_to_all(
+        jnp.tile(pivot_basis, repeats), "row", split_axis=1, concat_axis=1, tiled=True
+    )
     pivot_width = pivot_basis.shape[3]
     grouped = all_pivots.reshape(local_cols, cols_grid, rank_max, pivot_width)
     products = jnp.einsum(

time: 820 us -> 762 us (0.929)
  waiting for transfers between devices: 634 us -> 541 us
  blocking collectives: 0 us -> 31.9 us
    psum x3, waiting for transfers between devices: 217 us -> 160 us  [spread_2(): return lax.psum(jnp.where(mine, x, jnp.zeros_like(x)), axis)]
    all_to_all x0 -> x1, blocking collectives: none -> 31.9 us  [per_device(): lax.all_to_all(jnp.tile(pivot_basis, repeats), 'row', split_axis=1, conca...]
    all_gather x1 -> x0, waiting for transfers between devices: 29.4 us -> none  [per_device(): all_pivots = lax.all_gather(pivot_basis, 'row', axis=1, tiled=True)]
  transfers between devices with their start and end apart: 12 -> 11, of which waited for: 12 -> 10; matrix products, arithmetic and copies ran while one was open for 2% -> 2% of each run, Pallas kernels for 0% -> 0%
where the time goes in v1:
time: 762 us; the launch traced here: 752 us
  waiting for transfers between devices  541 us (71%)
  matrix products  65.4 us (9%)
  local copies, waits for them, and re-layouts  64.7 us (8%)
  blocking collectives  31.9 us (4%)
  other arithmetic  29.2 us (4%)
  between operations  16.2 us (2%)
    ppermute x7, waiting for transfers between devices, from_behind(): return lax.ppermute(x, axis, [(i, (i + by) % count) for i in range(count)])  299 us
    psum x3, waiting for transfers between devices, spread_2(): return lax.psum(jnp.where(mine, x, jnp.zeros_like(x)), axis)  160 us
    reduce_scatter x1, waiting for transfers between devices, per_device(): lax.psum_scatter(products.reshape(lax.axis_size('col') * local_cols, loca...  81.4 us
    all_to_all x1, blocking collectives, per_device(): lax.all_to_all(jnp.tile(pivot_basis, repeats), 'row', split_axis=1, conca...  31.9 us
    dot_general x1, matrix products, per_device(): jnp.einsum('axq,byq->abxy', scaled, col_panel, precision=highest, preferr...  18 us
    transpose x1, local copies, waits for them, and re-layouts, per_device(): jnp.einsum('trp,scup->cstru', own_pivots, grouped, precision=highest, pre...  17.6 us
    dot_general x1, matrix products, per_device(): jnp.einsum('trp,scup->cstru', own_pivots, grouped, precision=highest, pre...  15.9 us
  transfers between devices with their start and end apart: 11, of which 10 were waited for; matrix products, arithmetic and copies ran while one was open for 2% of the time, Pallas kernels for 0%

profile of v1, /device:TPU:0, one launch (start us, length us, event | category | flops | bytes accessed | tf_op | source)
XLA Modules:
  0.0 752.4 jit_solution(18433498306031218819)
XLA Ops:
  7.4 1.3 tile.10
  8.7 31.9 %all_to_all.5 = f32[8,8,64,128]{3,2,0,1:T(8,128)S(1)} all-to-all(f32[8,8,64,128]{3,2,0,1:T(8,128)S(1)} %tile.10), channel_id=1, replica_groups=mesh['row'=8,'col'=16] {'row'}, dimensions={1} | all-to-all | bytes 4194304 | tf_op jit(solution)/shard_map/all_to_all | solution.py:68
  40.8 0.7 copy-done.4
  41.5 15.9 %convolution_bitcast_fusion = f32[16,4,8,64,64]{3,4,2,0,1:T(8,128)} fusion(f32[4,16,64,128,1]{3,2,4,1,0:T(8,128)S(1)} %bitcast.104, f32[8,1,64,128]{3,2,1,0:T(8,128)S(1)} %copy-done.4), kind=kOutput, calls=%fused_computation.1 | convolution fusion | flops 3221225472 | bytes 10747904 | tf_op jit(solution)/shard_map/trp,scup->cstru/dot_general | solution.py:73
  57.3 17.6 %copy.49 = f32[16,4,8,64,64]{4,3,2,1,0:T(8,128)} copy(f32[16,4,8,64,64]{3,4,2,0,1:T(8,128)} %convolution_bitcast_fusion) | data formatting | bytes 16777216 | tf_op jit(solution)/shard_map/trp,scup->cstru/transpose | solution.py:73
  75.0 14.7 %reshape.471 = f32[64,8,4096]{2,1,0:T(8,128)} reshape(f32[16,4,8,64,64]{4,3,2,1,0:T(8,128)} %copy.49) | data formatting | bytes 16777216 | tf_op jit(solution)/shard_map/reshape | solution.py:81
  89.8 0.8 copy-done.8
  90.7 0.7 fusion.15
  92.0 1.8 copy.46
  93.8 81.4 %reduce-scatter.2.cloned.1.call-done = f32[4,8,4096]{2,1,0:T(8,128)} async-done(((f32[64,8,4096]{2,1,0:T(8,128)}), f32[4,8,4096]{2,1,0:T(8,128)}) %reduce-scatter.2.cloned.1.call-update) | async-done | bytes 524304 | tf_op jit(solution)/shard_map/reduce_scatter | solution.py:80
  175.3 1.5 reshape.472
  176.7 2.9 fusion.13
  179.6 3.9 fusion.9
  184.0 26.3 %collective-permute-done = f32[8,4,128,128]{2,3,0,1:T(8,128)} collective-permute-done((f32[8,4,128,128]{2,3,0,1:T(8,128)S(1)}, f32[8,4,128,128]{2,3,0,1:T(8,128)}, u32[]{:S(2)}, u32[]{:S(2)}) %collective-permute-start) | collective-permute-done | bytes 2097184 | tf_op jit(solution)/shard_map/ppermute | solution.py:17
  210.3 1.9 broadcast_select_fusion.1
  212.3 0.3 collective-permute-start.1
  212.6 46.3 %collective-permute-done.1 = f32[8,4,128,128]{2,3,0,1:T(8,128)S(1)} collective-permute-done((f32[8,4,128,128]{2,3,0,1:T(8,128)S(1)}, f32[8,4,128,128]{2,3,0,1:T(8,128)S(1)}, u32[]{:S(2)}, u32[]{:S(2)}) %collective-permute-start.1) | collective-permute-done | bytes 2097184 | tf_op jit(solution)/shard_map/ppermute | solution.py:17
  258.9 0.4 broadcast_select_fusion.2
  259.3 1.6 collective-permute-start.2
  260.9 44.4 %collective-permute-done.2 = f32[8,4,128,128]{2,3,0,1:T(8,128)S(1)} collective-permute-done((f32[8,4,128,128]{2,3,0,1:T(8,128)S(1)}, f32[8,4,128,128]{2,3,0,1:T(8,128)S(1)}, u32[]{:S(2)}, u32[]{:S(2)}) %collective-permute-start.2) | collective-permute-done | bytes 2097184 | tf_op jit(solution)/shard_map/ppermute | solution.py:17
  305.3 0.4 broadcast_select_fusion.3
  305.7 1.9 collective-permute-start.3
  307.7 46.5 %collective-permute-done.3 = f32[8,4,128,128]{2,3,0,1:T(8,128)S(1)} collective-permute-done((f32[8,4,128,128]{2,3,0,1:T(8,128)S(1)}, f32[8,4,128,128]{2,3,0,1:T(8,128)S(1)}, u32[]{:S(2)}, u32[]{:S(2)}) %collective-permute-start.3) | collective-permute-done | bytes 2097184 | tf_op jit(solution)/shard_map/ppermute | solution.py:17
  354.1 0.4 broadcast_select_fusion.4
  354.6 49.8 %collective-permute-done.4 = f32[8,4,128,128]{2,3,0,1:T(8,128)S(1)} collective-permute-done((f32[8,4,128,128]{2,3,0,1:T(8,128)S(1)}, f32[8,4,128,128]{2,3,0,1:T(8,128)S(1)}, u32[]{:S(2)}, u32[]{:S(2)}) %collective-permute-start.4) | collective-permute-done | bytes 2097184 | tf_op jit(solution)/shard_map/ppermute | solution.py:17
  404.4 0.4 broadcast_select_fusion.5
  404.9 59.5 %collective-permute-done.5 = f32[8,4,128,128]{2,3,0,1:T(8,128)S(1)} collective-permute-done((f32[8,4,128,128]{2,3,0,1:T(8,128)S(1)}, f32[8,4,128,128]{2,3,0,1:T(8,128)S(1)}, u32[]{:S(2)}, u32[]{:S(2)}) %collective-permute-start.5) | collective-permute-done | bytes 2097184 | tf_op jit(solution)/shard_map/ppermute | solution.py:17
  464.4 0.3 broadcast_select_fusion.6
  466.0 26.5 %collective-permute-done.6 = f32[8,4,128,128]{2,3,0,1:T(8,128)} collective-permute-done((f32[8,4,128,128]{2,3,0,1:T(8,128)S(1)}, f32[8,4,128,128]{2,3,0,1:T(8,128)}, u32[]{:S(2)}, u32[]{:S(2)}) %collective-permute-start.6) | collective-permute-done | bytes 2097184 | tf_op jit(solution)/shard_map/ppermute | solution.py:17
  492.5 3.2 broadcast_select_fusion.7
  495.7 2.0 copy.51
  497.8 1.9 fusion.21
  499.7 13.0 %bitcast_add_fusion = f32[16,8,128,128]{3,1,2,0:T(8,128)S(1)} fusion(f32[16,1,8,1,128,128]{5,4,3,2,1,0:T(8,128)} %param.9, f32[16,4,128,128]{3,0,2,1:T(8,128)S(1)} %fusion.21, s32[4]{0:T(128)S(1)} %and_select_fusion), kind=kOutput, calls=%fused_computation.3 | convolution fusion | flops 102760480 | bytes 20971536 | tf_op jit(solution)/shard_map/bs,asxy->abxy/dot_general | solution.py:130
  512.7 1.2 broadcast.770
  513.9 5.8 broadcast_select_fusion
  519.7 1.1 select_bitcast_fusion.2
  520.8 1.6 select_bitcast_fusion
  522.6 104.6 %all-reduce.9.cloned.1.call-done = (f32[16,128,128]{2,1,0:T(8,128)}, f32[16,128,128]{2,1,0:T(8,128)}, f32[16,128,128]{2,1,0:T(8,128)}, f32[16,128,128]{2,1,0:T(8,128)}) async-done(((f32[16,128,128]{2,1,0:T(8,128)}, f32[16,128,128]{2,1,0:T(8,128)}, f32[16,128,128]{2,1,0:T(8,128)}, f32[16,128,128]{2,1,0:T(8,128)}), (f32[16,128,128]{2,1,0:T(8,128)}, f32[16,128,128]{2,1,0:T(8,128)}, f32[16,128,128]{2,1,0:T(8,128)}, ...) | async-done | bytes 4194320 | tf_op jit(solution)/shard_map/psum | solution.py:12
  627.2 1.5 constant_dynamic-update-slice_fusion.3
  629.2 0.9 copy-done.5
  630.2 2.0 copy-done.2
  632.2 1.6 fusion.7
  633.9 9.8 %fusion.10 = f32[16,128,512]{2,1,0:T(8,128)} fusion(f32[16,128,512]{2,1,0:T(8,128)} %copy-done.2, f32[512,512]{1,0:T(8,128)S(1)} %copy-done), kind=kOutput, calls=%fused_computation.14 | convolution fusion | flops 6442450944 | bytes 9437184 | tf_op jit(solution)/shard_map/axp,pq->axq/dot_general | solution.py:142
  643.7 55.2 %all-reduce.7.cloned.1.call-done = f32[8,128,512]{2,1,0:T(8,128)} async-done(((f32[8,128,512]{2,1,0:T(8,128)}), f32[8,128,512]{2,1,0:T(8,128)}) %all-reduce.7.cloned.1.call-update) | async-done | bytes 2097168 | tf_op jit(solution)/shard_map/psum | solution.py:12
  698.9 18.0 %fusion.1 = f32[8,128,16,128]{3,1,2,0:T(8,128)} fusion(f32[16,128,512]{2,1,0:T(8,128)} %fusion.10, f32[8,128,512]{2,1,0:T(8,128)} %all-reduce.7.cloned.1.call-done), kind=kOutput, calls=%fused_computation.4 | convolution fusion | flops 12884901888 | bytes 14680064 | tf_op jit(solution)/shard_map/axq,byq->abxy/dot_general | solution.py:149
  716.9 9.4 %copy.58 = f32[8,128,16,128]{1,0,3,2:T(8,128)} copy(f32[8,128,16,128]{3,1,2,0:T(8,128)} %fusion.1) | data formatting | bytes 16777216 | tf_op jit(solution)/shard_map/axq,byq->abxy/dot_general | solution.py:149
  726.4 10.2 %fusion = f32[16,1,8,1,128,128]{5,2,4,0,3,1:T(8,128)} fusion(f32[16,8,128,128]{3,1,2,0:T(8,128)} %copy-done.1, f32[8,128,16,128]{1,0,3,2:T(8,128)} %copy.58, pred[16,8]{1,0:T(8,128)(4,1)S(1)} %compare_and_fusion), kind=kLoop, calls=%fused_computation.2 | loop fusion | flops 4194304 | bytes 25165952 | tf_op jit(solution)/shard_map/broadcast_in_dim | solution.py:156
  736.5 8.2 %copy.59 = f32[16,1,8,1,128,128]{5,4,3,2,1,0:T(8,128)} copy(f32[16,1,8,1,128,128]{5,2,4,0,3,1:T(8,128)} %fusion) | data formatting | bytes 16777216 | tf_op jit(solution)/shard_map/broadcast_in_dim | solution.py:156
  (58 shorter events, 3.0 us)
Async XLA Ops:
  7.4 626.5 %copy-start = (f32[512,512]{1,0:T(8,128)S(1)}, f32[512,512]{1,0:T(8,128)}, u32[]{:S(2)}) copy-start(f32[512,512]{1,0:T(8,128)} %param.15) | copy-start | bytes 3145732
  7.4 167.9 %reduce-scatter.2.cloned.1.call-start = ((), (), s32[]{:S(2)}) async-start(), calls=%async_computation.3 | async-start | bytes 8912896 | tf_op jit(solution)/shard_map/reduce_scatter | solution.py:80
  40.5 1.0 copy-start.4
  89.7 0.9 copy-start.8
  89.7 1.8 copy-start.9
  89.7 2.3 copy-start.3
  89.7 89.9 %all-reduce.5.cloned.1.call-start = ((), (), s32[]{:S(2)}) async-start(), calls=%async_computation.2 | async-start | bytes 262144 | tf_op jit(solution)/shard_map/psum | solution.py:12
  91.4 535.9 %all-reduce.9.cloned.1.call-start = ((), (), s32[]{:S(2)}) async-start(), calls=%async_computation.5 | async-start | bytes 8388608 | tf_op jit(solution)/shard_map/psum | solution.py:12
  179.6 4.0 copy-start.10
  183.6 26.8 %collective-permute-start = (f32[8,4,128,128]{2,3,0,1:T(8,128)S(1)}, f32[8,4,128,128]{2,3,0,1:T(8,128)}, u32[]{:S(2)}, u32[]{:S(2)}) collective-permute-start(f32[8,4,128,128]{2,3,0,1:T(8,128)S(1)} %fusion.9), channel_id=1, source_target_pairs={{0,16},{16,32},{32,48},{48,64},{64,80},{80,96},{96,112},{112,0},{1... | collective-permute-start | bytes 6291464 | tf_op jit(solution)/shard_map/ppermute | solution.py:17
  212.3 46.6 %collective-permute-start.1 = (f32[8,4,128,128]{2,3,0,1:T(8,128)S(1)}, f32[8,4,128,128]{2,3,0,1:T(8,128)S(1)}, u32[]{:S(2)}, u32[]{:S(2)}) collective-permute-start(f32[8,4,128,128]{2,3,0,1:T(8,128)S(1)} %broadcast_select_fusion.1), channel_id=1, source_target_pairs={{0,32},{16,48},{32,64},{48,80},{64,96},{80,112},{96,0},{112,16},{1... | collective-permute-start | bytes 6291464 | tf_op jit(solution)/shard_map/ppermute | solution.py:17
  259.3 46.0 %collective-permute-start.2 = (f32[8,4,128,128]{2,3,0,1:T(8,128)S(1)}, f32[8,4,128,128]{2,3,0,1:T(8,128)S(1)}, u32[]{:S(2)}, u32[]{:S(2)}) collective-permute-start(f32[8,4,128,128]{2,3,0,1:T(8,128)S(1)} %broadcast_select_fusion.2), channel_id=1, source_target_pairs={{0,64},{16,80},{32,96},{48,112},{64,0},{80,16},{96,32},{112,48},{1... | collective-permute-start | bytes 6291464 | tf_op jit(solution)/shard_map/ppermute | solution.py:17
  305.7 48.4 %collective-permute-start.3 = (f32[8,4,128,128]{2,3,0,1:T(8,128)S(1)}, f32[8,4,128,128]{2,3,0,1:T(8,128)S(1)}, u32[]{:S(2)}, u32[]{:S(2)}) collective-permute-start(f32[8,4,128,128]{2,3,0,1:T(8,128)S(1)} %broadcast_select_fusion.3), channel_id=1, source_target_pairs={{0,1},{1,2},{2,3},{3,4},{4,5},{5,6},{6,7},{7,8},{8,9},{9,10},{10,1... | collective-permute-start | bytes 6291464 | tf_op jit(solution)/shard_map/ppermute | solution.py:17
  354.5 49.9 %collective-permute-start.4 = (f32[8,4,128,128]{2,3,0,1:T(8,128)S(1)}, f32[8,4,128,128]{2,3,0,1:T(8,128)S(1)}, u32[]{:S(2)}, u32[]{:S(2)}) collective-permute-start(f32[8,4,128,128]{2,3,0,1:T(8,128)S(1)} %broadcast_select_fusion.4), channel_id=1, source_target_pairs={{0,2},{1,3},{2,4},{3,5},{4,6},{5,7},{6,8},{7,9},{8,10},{9,11},{10,... | collective-permute-start | bytes 6291464 | tf_op jit(solution)/shard_map/ppermute | solution.py:17
  404.8 59.6 %collective-permute-start.5 = (f32[8,4,128,128]{2,3,0,1:T(8,128)S(1)}, f32[8,4,128,128]{2,3,0,1:T(8,128)S(1)}, u32[]{:S(2)}, u32[]{:S(2)}) collective-permute-start(f32[8,4,128,128]{2,3,0,1:T(8,128)S(1)} %broadcast_select_fusion.5), channel_id=1, source_target_pairs={{0,4},{1,5},{2,6},{3,7},{4,8},{5,9},{6,10},{7,11},{8,12},{9,13},{1... | collective-permute-start | bytes 6291464 | tf_op jit(solution)/shard_map/ppermute | solution.py:17
  464.8 27.7 %collective-permute-start.6 = (f32[8,4,128,128]{2,3,0,1:T(8,128)S(1)}, f32[8,4,128,128]{2,3,0,1:T(8,128)}, u32[]{:S(2)}, u32[]{:S(2)}) collective-permute-start(f32[8,4,128,128]{2,3,0,1:T(8,128)S(1)} %broadcast_select_fusion.6), channel_id=1, source_target_pairs={{0,8},{1,9},{2,10},{3,11},{4,12},{5,13},{6,14},{7,15},{8,0},{9,1},... | collective-permute-start | bytes 6291464 | tf_op jit(solution)/shard_map/ppermute | solution.py:17
  512.7 7.0 copy-start.1
  522.4 176.6 %all-reduce.7.cloned.1.call-start = ((), (), s32[]{:S(2)}) async-start(), calls=%async_computation.4 | async-start | bytes 4194304 | tf_op jit(solution)/shard_map/psum | solution.py:12
  627.2 1.5 copy-start.7
  627.2 1.9 copy-start.6
  628.8 1.3 copy-start.5
  630.2 2.0 copy-start.2
Sparse Core Ops, SparseCore 0:
  89.9 85.3 reduce-scatter.1
  522.5 104.6 all-reduce.8
Sparse Core Ops, SparseCore 1:
  92.5 60.8 all-reduce.4
  633.9 65.0 all-reduce.6
